TPU v7x, 256 devices: a whole 4x4x8 slice. The times are simulated.
256 devices in a mesh: pair: 4 (over y_lo, core), col: 64 (over y_hi, x, z).
Axes of the slice: x: 4, y: 4 (y_hi: 2, y_lo: 2; y = y_hi * 2 + y_lo), z: 8, core: 2. Of those that a mesh axis runs over, the one named last changes fastest.
Arguments:
- amplitudes: bfloat16 [1536, 4096], P('pair', 'col'), may hold values from -6 to 6
- integrals: bfloat16 [4096, 81920], P('pair', 'col'), may hold values from -0.25 to 0.25
- irrep_start: int32 [9], replicated, may hold values from 0 to 4096, as said below
- pair_irrep: int32 [1536], P('pair'), may hold values from 0 to 7
Outputs:
- ladder: bfloat16 [1536, 81920], P('pair', 'col')
Inputs may be any that keep to these rules, and one draw needn't show every extreme that they name: Strictly rising multiples of 128; the first is 0 and the last is 4096; irrep j owns rows irrep_start[j] to irrep_start[j+1] - 1.
All inputs are finite; a program needn't handle non-finite values.
Results may differ from a plain program's by a relative error of at most 0.001.
Values may be sent and summed in bfloat16 or wider, within the bound.
A program may use at most 64 MiB of HBM per device.

v0:
```python
import jax
import jax.numpy as jnp
from jax import lax
from jax.sharding import PartitionSpec as P


def per_device(amplitudes, integrals, irrep_start, pair_irrep):
    local_rows = amplitudes.shape[1]
    first_row = lax.axis_index("col") * local_rows
    rows = first_row + jnp.arange(local_rows, dtype=jnp.int32)
    row_irrep = jnp.sum((rows[:, None] >= irrep_start[None, 1:8]).astype(jnp.int32), axis=1)
    keep = pair_irrep[:, None] == row_irrep[None, :]
    masked = jnp.where(keep, amplitudes, jnp.zeros_like(amplitudes))
    full_amp = lax.all_gather(masked, "col", axis=1, tiled=True)
    blocks = lax.all_to_all(full_amp, "pair", split_axis=1, concat_axis=0, tiled=True)
    summed = lax.psum_scatter(
        jnp.dot(blocks, integrals, preferred_element_type=jnp.float32),
        "pair",
        scatter_dimension=0,
        tiled=True,
    )
    return summed.astype(jnp.bfloat16)


def solution(mesh):
    placed = (P("pair", "col"), P("pair", "col"), P(), P("pair"))
    return jax.shard_map(
        per_device, mesh=mesh, in_specs=placed, out_specs=P("pair", "col"), check_vma=False
    )
```

profile of v0, /device:TPU:2, one launch (start us, length us, event | category | flops | bytes accessed | tf_op | source)
XLA Modules:
  0.0 276.4 jit_solution(218470783332346924)
XLA Ops:
  6.5 0.0 copy-start
  6.5 0.0 all-gather.2.cloned.1.call-start
  6.5 0.9 slice.3
  7.4 0.1 convert_reduce_fusion
  7.5 1.5 compare_select_fusion
  9.0 0.0 all-gather.2.cloned.1.call-update
  9.0 0.0 reduce-scatter.2.cloned.1.call-start
  9.1 127.7 %all-gather.2.cloned.1.call-done = bf16[384,4096]{0,1:T(8,128)(2,1)} async-done(((bf16[384,64]{0,1:T(8,128)(2,1)}), bf16[384,4096]{0,1:T(8,128)(2,1)}) %all-gather.2.cloned.1.call-update) | async-done | bytes 3145744 | tf_op jit(solution)/shard_map/all_gather | solution.py:14
  136.8 42.2 %all_to_all.19 = bf16[384,4,1024]{0,2,1:T(8,128)(2,1)} all-to-all(bf16[384,4,1024]{0,2,1:T(8,128)(2,1)} %bitcast.6), channel_id=1, replica_groups=mesh['pair'=4,'col'=64] {'pair'}, dimensions={1} | all-to-all | bytes 6291456 | tf_op jit(solution)/shard_map/all_to_all | solution.py:15
  179.0 4.7 %copy.6 = bf16[4,384,1024]{2,1,0:T(8,128)(2,1)} copy(bf16[4,384,1024]{1,2,0:T(8,128)(2,1)} %bitcast.5) | data formatting | bytes 6291456 | tf_op jit(solution)/shard_map/all_to_all | solution.py:15
  183.8 0.0 copy-done
  183.8 9.2 %fusion = f32[1536,1280]{1,0:T(8,128)} fusion(bf16[1536,1024]{1,0:T(8,128)(2,1)} %bitcast.7, bf16[1024,1280]{1,0:T(8,128)(2,1)S(1)} %copy-done), kind=kOutput, calls=%fused_computation.3 | convolution fusion | flops 4026531840 | bytes 13631488 | tf_op jit(solution)/shard_map/dot_general | solution.py:17
  193.0 0.0 reduce-scatter.2.cloned.1.call-update
  193.0 74.0 %reduce-scatter.2.cloned.1.call-done = f32[384,1280]{1,0:T(8,128)} async-done(((f32[1536,1280]{1,0:T(8,128)}), f32[384,1280]{1,0:T(8,128)}) %reduce-scatter.2.cloned.1.call-update) | async-done | bytes 1966096 | tf_op jit(solution)/shard_map/reduce_scatter | solution.py:16
  267.0 2.6 convert_element_type.7
  (1 shorter events, 0.0 us)
Async XLA Ops:
  6.5 177.2 %copy-start = (bf16[1024,1280]{1,0:T(8,128)(2,1)S(1)}, bf16[1024,1280]{1,0:T(8,128)(2,1)}, u32[]{:S(2)}) copy-start(bf16[1024,1280]{1,0:T(8,128)(2,1)} %param.5) | copy-start | bytes 7864324
  6.5 130.3 %all-gather.2.cloned.1.call-start = ((), (), s32[]{:S(2)}) async-start(), calls=%async_computation.2 | async-start | bytes 3194880 | tf_op jit(solution)/shard_map/all_gather | solution.py:14
  9.0 257.9 %reduce-scatter.2.cloned.1.call-start = ((), (), s32[]{:S(2)}) async-start(), calls=%async_computation.3 | async-start | bytes 9830400 | tf_op jit(solution)/shard_map/reduce_scatter | solution.py:16
Sparse Core Ops, SparseCore 0:
  11.0 125.7 all-gather.1
  193.2 73.7 reduce-scatter.1
where the time goes:
time: 278 us; the launch traced here: 276 us
  waiting for transfers between devices  202 us (73%)
  blocking collectives  42.2 us (15%)
  between operations  13.4 us (5%)
  matrix products  9.23 us (3%)
  local copies, waits for them, and re-layouts  5.62 us (2%)
  other arithmetic  4.18 us (2%)
    all_gather x1, waiting for transfers between devices, per_device(): full_amp = lax.all_gather(masked, 'col', axis=1, tiled=True)  128 us
    reduce_scatter x1, waiting for transfers between devices, per_device(): lax.psum_scatter(jnp.dot(blocks, integrals, preferred_element_type=jnp.fl...  74 us
    all_to_all x1, blocking collectives, per_device(): lax.all_to_all(full_amp, 'pair', split_axis=1, concat_axis=0, tiled=True)  42.2 us
    dot_general x1, matrix products, per_device(): jnp.dot(blocks, integrals, preferred_element_type=jnp.float32)  9.23 us
  transfers between devices with their start and end apart: 2, of which 2 were waited for; matrix products, arithmetic and copies ran while one was open for 0% of the time, Pallas kernels for 0%

commit v1 on v0

v1 whole, which is shorter than its diff:
```python
import functools

import jax
import jax.numpy as jnp
from jax import lax
from jax.experimental import pallas as pl
from jax.experimental.pallas import tpu as pltpu
from jax.sharding import PartitionSpec as P

MESH = pl.DeviceIdType.MESH
NX, NZ = 4, 8
TILE = 256
F32 = jnp.float32


def iota(shape, axis):
    return lax.broadcasted_iota(jnp.int32, shape, axis)


def kernel(
    cap, slots,
    start_ref, irr_ref, amp_ref, int_ref,
    out_ref, flag_ref,
    irr_all, comp, gat, ints, pick, lhs, own, mix, low, acc, sendb, recvb,
    irr_send, irr_recv, yx_send, yx_recv, z_send, z_recv, int_send, int_recv, own_sem, ex_send, ex_recv,
):
    pairs = irr_ref.shape[1]
    depth, cols = int_ref.shape
    rows = amp_ref.shape[0]
    half = 2 * depth
    tiles = cols // TILE

    pair = lax.axis_index("pair")
    col = lax.axis_index("col")
    h, core = pair // 2, pair % 2
    yh, x, z = col // (NX * NZ), (col // NZ) % NX, col % NZ
    kind = (h == yh).astype(jnp.int32)
    selfish = h == yh

    def at(hh, cc, yy, xx, zz):
        return (hh * 2 + cc, (yy * NX + xx) * NZ + zz)

    def signal(dev):
        pl.semaphore_signal(barrier, inc=1, device_id=dev, device_id_type=MESH)

    barrier = pltpu.get_barrier_semaphore()
    relations = ((0, 1), (1, 0), (1, 1))
    for dh, dc in relations:
        signal(at((h + dh) % 2, (core + dc) % 2, yh, x, z))
    signal(at(h, core, yh, x, (z + 1) % NZ))
    signal(at(h, core, yh, x, (z + NZ - 1) % NZ))
    for u in range(2):
        for dx in range(NX):
            source = at(u, core, h, (x + dx) % NX, z)
            if dx == 0:
                @pl.when(jnp.logical_not(jnp.logical_and(selfish, u == h)))
                def _(source=source):
                    signal(source)
            else:
                signal(source)

    own_copy = pltpu.make_async_copy(int_ref, ints.at[pl.ds(core * depth, depth)], own_sem)
    own_copy.start()

    def row_irrep(row):
        total = jnp.int32(0)
        for j in range(1, 8):
            total = total + (row >= start_ref[j]).astype(jnp.int32)
        return total

    eye = iota((pairs, pairs), 0) == iota((pairs, pairs), 1)
    below = iota((pairs, pairs), 1) < iota((pairs, pairs), 0)
    above = iota((pairs, pairs), 0) < iota((pairs, pairs), 1)

    def down(v):
        return jnp.sum(jnp.where(eye, v, 0.0), axis=1, keepdims=True)

    def touch(v, which):
        total = jnp.zeros_like(v)
        for r in range(8):
            meets = jnp.logical_and(start_ref[r] < half * (which + 1), start_ref[r + 1] > half * which)
            total = total + jnp.where(v == float(r), jnp.where(meets, 1.0, 0.0), 0.0)
        return total

    mine_l = irr_ref[...].astype(F32)
    mine_s = down(mine_l)
    rank_s = jnp.sum(jnp.where(jnp.logical_and(below, mine_s == mine_l), 1.0, 0.0), axis=1, keepdims=True)
    here = row_irrep(col * rows).astype(F32)
    where_s = jnp.where(mine_s == here, rank_s, -1.0)
    chosen = jnp.where(where_s == iota((pairs, cap), 1).astype(F32), 1.0, 0.0).astype(jnp.bfloat16)
    block = jnp.dot(amp_ref[...], chosen, preferred_element_type=F32).astype(jnp.bfloat16)
    comp[...] = block

    @pl.when(selfish)
    def _():
        gat[1, z, x] = block

    pick_own = (mine_s * 512.0 + rank_s).astype(jnp.int32) - iota((pairs, cap), 1)

    n_targets = 5 + 2 * NX - kind
    pl.semaphore_wait(barrier, n_targets)

    def yx_copy(u, dx):
        return pltpu.make_async_remote_copy(
            src_ref=comp, dst_ref=gat.at[kind, z, x],
            send_sem=yx_send.at[u * NX + dx], recv_sem=yx_recv.at[kind, x],
            device_id=at(yh, core, u, (x + dx) % NX, z), device_id_type=MESH,
        )

    def not_self(u, dx, act):
        if dx == 0:
            @pl.when(jnp.logical_not(jnp.logical_and(selfish, u == yh)))
            def _():
                act()
        else:
            act()

    for dx in (2, 1, 3, 0):
        for u in range(2):
            not_self(u, dx, lambda u=u, dx=dx: yx_copy(u, dx).start())

    def irr_copy(k):
        dh, dc = relations[k]
        return pltpu.make_async_remote_copy(
            src_ref=irr_ref, dst_ref=irr_all.at[pair],
            send_sem=irr_send.at[k], recv_sem=irr_recv.at[k],
            device_id=at((h + dh) % 2, (core + dc) % 2, yh, x, z), device_id_type=MESH,
        )

    for k in range(3):
        irr_copy(k).start()

    int_copy = pltpu.make_async_remote_copy(
        src_ref=int_ref, dst_ref=ints.at[pl.ds(core * depth, depth)],
        send_sem=int_send, recv_sem=int_recv,
        device_id=at(h, 1 - core, yh, x, z), device_id_type=MESH,
    )
    int_copy.start()

    def z_copy(t, d, s, q):
        step = 1 if d == 0 else NZ - 1
        slab = (z + NZ * NZ - (s - 1) * step) % NZ
        piece = gat.at[t, slab, pl.ds(2 * q, 2)]
        return pltpu.make_async_remote_copy(
            src_ref=piece, dst_ref=piece,
            send_sem=z_send.at[t, d, s - 1, q], recv_sem=z_recv.at[t, d, s - 1, q],
            device_id=at(h, core, yh, x, (z + step) % NZ), device_id_type=MESH,
        )

    def z_arrival(t, d, s, q):
        step = 1 if d == 0 else NZ - 1
        slab = (z + NZ * NZ - s * step) % NZ
        piece = gat.at[t, slab, pl.ds(2 * q, 2)]
        return pltpu.make_async_remote_copy(
            src_ref=piece, dst_ref=piece,
            send_sem=z_send.at[t, d, s - 1, q], recv_sem=z_recv.at[t, d, s - 1, q],
            device_id=at(h, core, yh, x, (z + step) % NZ), device_id_type=MESH,
        )

    z_steps = [(s, d, q) for s in range(1, 5) for q in range(2) for d in range(2) if s < 4 or q == d]

    def gather_start(t):
        for dx in range(NX):
            xx = (x + dx) % NX
            arrival = pltpu.make_async_remote_copy(
                src_ref=comp, dst_ref=gat.at[t, z, xx],
                send_sem=yx_send.at[0], recv_sem=yx_recv.at[t, xx],
                device_id=at(h, core, yh, xx, z), device_id_type=MESH,
            )
            if t == 1 and dx == 0:
                @pl.when(jnp.logical_not(selfish))
                def _(arrival=arrival):
                    arrival.wait_recv()
            else:
                arrival.wait_recv()
        for s, d, q in z_steps:
            if s == 1:
                z_copy(t, d, 1, q).start()

    def gather_rest(t):
        for s, d, q in z_steps:
            if s > 1:
                z_arrival(t, d, s - 1, q).wait_recv()
                z_copy(t, d, s, q).start()
        for s, d, q in z_steps:
            if (s + 1, d, q) not in z_steps:
                z_arrival(t, d, s, q).wait_recv()

    gather_start(0)

    for k in range(3):
        dh, dc = relations[k]
        arrival = pltpu.make_async_remote_copy(
            src_ref=irr_ref, dst_ref=irr_all.at[((h + dh) % 2) * 2 + (core + dc) % 2],
            send_sem=irr_send.at[k], recv_sem=irr_recv.at[k],
            device_id=at((h + dh) % 2, (core + dc) % 2, yh, x, z), device_id_type=MESH,
        )
        arrival.wait_recv()

    theirs_l = irr_all[(1 - h) * 2 + core].astype(F32)
    theirs_s = down(theirs_l)
    rank_l = jnp.sum(jnp.where(jnp.logical_and(above, theirs_s == theirs_l), 1.0, 0.0), axis=0, keepdims=True)
    key_l = theirs_l * 512.0 + rank_l + 1.0
    src_l = touch(theirs_l, h)
    both_l = src_l * touch(theirs_l, 1 - h)
    src_s, both_s = down(src_l), down(both_l)
    pos1 = jnp.sum(jnp.where(above, src_s, 0.0), axis=0, keepdims=True)
    pos2 = jnp.sum(src_l, axis=1, keepdims=True) + jnp.sum(jnp.where(above, both_s, 0.0), axis=0, keepdims=True)
    pos1 = jnp.where(src_l > 0.0, pos1, -1.0)
    pos2 = jnp.where(both_l > 0.0, pos2, -1.0)
    slot = iota((slots, pairs), 0).astype(F32)
    is_low = pos2 == slot
    key_slot = jnp.sum(jnp.where(jnp.logical_or(pos1 == slot, is_low), key_l, 0.0), axis=1, keepdims=True)
    low[...] = jnp.sum(jnp.where(is_low, 1.0, 0.0), axis=1, keepdims=True)
    pick[...] = (key_slot - 1.0).astype(jnp.int32) - iota((slots, cap), 1)

    gather_rest(0)

    def expand(t, keys, dst):
        for b in range(half // 128):
            here = row_irrep(h * half + b * 128) * 512
            one_hot = jnp.where(keys == here, 1.0, 0.0).astype(jnp.bfloat16)
            zz, xx = 2 * (b % (NZ // 2)), b // (NZ // 2)
            packed = jnp.concatenate([gat[t, zz, xx], gat[t, zz + 1, xx]], axis=0)
            part = lax.dot_general(one_hot, packed, (((1,), (1,)), ((), ())), preferred_element_type=F32)
            dst[:, pl.ds(b * 128, 128)] = part.astype(jnp.bfloat16)

    expand(0, pick[...], lhs)
    own_copy.wait()
    int_copy.wait_recv()

    def ex_copy(j):
        return pltpu.make_async_remote_copy(
            src_ref=sendb.at[j], dst_ref=recvb.at[j],
            send_sem=ex_send.at[j], recv_sem=ex_recv.at[j],
            device_id=at(1 - h, core, yh, x, z), device_id_type=MESH,
        )

    @pl.loop(0, tiles + 1)
    def _(j):
        @pl.when(j < tiles)
        def _():
            part = jnp.dot(lhs[...], ints[:, pl.ds(pl.multiple_of(j * TILE, TILE), TILE)], preferred_element_type=F32)
            high = part.astype(jnp.bfloat16).astype(F32)
            sendb[j] = jnp.where(low[...] > 0.0, part - high, part).astype(jnp.bfloat16)

        @pl.when(j > 0)
        def _():
            ex_copy(j - 1).start()

    gather_start(1)
    src_l = touch(mine_l, 1 - h)
    both_l = src_l * touch(mine_l, h)
    src_s, both_s = down(src_l), down(both_l)
    pos1 = jnp.sum(jnp.where(below, src_l, 0.0), axis=1, keepdims=True)
    pos2 = jnp.sum(src_l, axis=1, keepdims=True) + jnp.sum(jnp.where(below, both_l, 0.0), axis=1, keepdims=True)
    pos1 = jnp.where(src_s > 0.0, pos1, -1.0)
    pos2 = jnp.where(both_s > 0.0, pos2, -1.0)
    slot = iota((pairs, slots), 1).astype(F32)
    mix[...] = jnp.where(jnp.logical_or(pos1 == slot, pos2 == slot), 1.0, 0.0).astype(jnp.bfloat16)

    fits = jnp.ones((1, 1), F32)
    for g in range(4):
        v = jnp.where(pair == g, mine_l, irr_all[g].astype(F32))
        for r in range(8):
            count = jnp.sum(jnp.where(v == float(r), 1.0, 0.0), axis=1, keepdims=True)
            fits = jnp.where(count > float(cap), 0.0, fits)
        src = touch(v, 1 - g // 2)
        need = jnp.sum(src + src * touch(v, g // 2), axis=1, keepdims=True)
        fits = jnp.where(need > float(slots), 0.0, fits)
    flag_ref[...] = jnp.broadcast_to(fits, flag_ref.shape)

    gather_rest(1)
    expand(1, pick_own, own)

    @pl.loop(0, tiles)
    def _(j):
        acc[j] = jnp.dot(own[...], ints[:, pl.ds(pl.multiple_of(j * TILE, TILE), TILE)], preferred_element_type=F32)

    @pl.loop(0, tiles)
    def _(j):
        ex_copy(j).wait_recv()
        total = acc[j] + jnp.dot(mix[...], recvb[j], preferred_element_type=F32)
        out_ref[:, pl.ds(pl.multiple_of(j * TILE, TILE), TILE)] = total.astype(jnp.bfloat16)

    for dx in range(NX):
        for u in range(2):
            not_self(u, dx, lambda u=u, dx=dx: yx_copy(u, dx).wait_send())
    for k in range(3):
        irr_copy(k).wait_send()
    int_copy.wait_send()
    for t in range(2):
        for s, d, q in z_steps:
            z_copy(t, d, s, q).wait_send()

    @pl.loop(0, tiles)
    def _(j):
        ex_copy(j).wait_send()


def ladder(cap, slots, collective_id, starts, irreps, amp, integrals):
    rows, pairs = amp.shape
    depth, cols = integrals.shape
    half, tiles = 2 * depth, cols // TILE
    bf16 = jnp.bfloat16
    dma = pltpu.SemaphoreType.DMA
    vmem = pl.BlockSpec(memory_space=pltpu.VMEM)
    return pl.pallas_call(
        functools.partial(kernel, cap, slots),
        out_shape=(jax.ShapeDtypeStruct((pairs, cols), bf16), jax.ShapeDtypeStruct((8, 128), F32)),
        in_specs=[pl.BlockSpec(memory_space=pltpu.SMEM), vmem, vmem, pl.BlockSpec(memory_space=pl.ANY)],
        out_specs=(vmem, vmem),
        scratch_shapes=[
            pltpu.VMEM((4, 1, pairs), jnp.int32),
            pltpu.VMEM((rows, cap), bf16),
            pltpu.VMEM((2, NZ, NX, rows, cap), bf16),
            pltpu.VMEM((half, cols), bf16),
            pltpu.VMEM((slots, cap), jnp.int32),
            pltpu.VMEM((slots, half), bf16),
            pltpu.VMEM((pairs, half), bf16),
            pltpu.VMEM((pairs, slots), bf16),
            pltpu.VMEM((slots, 1), F32),
            pltpu.VMEM((tiles, pairs, TILE), F32),
            pltpu.VMEM((tiles, slots, TILE), bf16),
            pltpu.VMEM((tiles, slots, TILE), bf16),
            dma((3,)), dma((3,)), dma((2 * NX,)), dma((2, NX)), dma((2, 2, 4, 2)), dma((2, 2, 4, 2)),
            dma, dma, dma, dma((tiles,)), dma((tiles,)),
        ],
        compiler_params=pltpu.CompilerParams(
            collective_id=collective_id, has_side_effects=True, vmem_limit_bytes=56 * 1024 * 1024
        ),
        name="ladder_" + str(slots),
    )(starts, irreps, amp, integrals)


def per_device(amplitudes, integrals, irrep_start, pair_irrep):
    pairs = amplitudes.shape[0]
    operands = (irrep_start, pair_irrep.reshape(1, pairs), amplitudes.T, integrals)
    out, fits = ladder(128, 448, 0, *operands)
    return lax.cond(
        fits[0, 0] > 0.0,
        lambda *_: out,
        lambda *args: ladder(pairs, 2 * pairs, 1, *args)[0],
        *operands,
    )


def solution(mesh):
    placed = (P("pair", "col"), P("pair", "col"), P(), P("pair"))
    return jax.shard_map(
        per_device, mesh=mesh, in_specs=placed, out_specs=P("pair", "col"), check_vma=False
    )
```

time: 278 us -> 56.3 us (0.20)
  waiting for transfers between devices: 202 us -> 0 us
  Pallas kernels: 0 us -> 51.5 us
  blocking collectives: 42.2 us -> 0 us
  between operations: 13.4 us -> 0.7 us
  matrix products: 9.23 us -> 0 us
  other arithmetic: 4.18 us -> 0 us
    all_gather x1 -> x0, waiting for transfers between devices: 128 us -> none  [per_device(): full_amp = lax.all_gather(masked, 'col', axis=1, tiled=True)]
    reduce_scatter x1 -> x0, waiting for transfers between devices: 74 us -> none  [per_device(): lax.psum_scatter(jnp.dot(blocks, integrals, preferred_element_type=jnp.fl...]
    pallas_call x0 -> x1, Pallas kernels: none -> 51.5 us  [ladder(): pl.pallas_call(functools.partial(kernel, cap, slots), out_shape=(jax.Shap...]
    all_to_all x1 -> x0, blocking collectives: 42.2 us -> none  [per_device(): lax.all_to_all(full_amp, 'pair', split_axis=1, concat_axis=0, tiled=True)]
    dot_general x1 -> x0, matrix products: 9.23 us -> none  [per_device(): jnp.dot(blocks, integrals, preferred_element_type=jnp.float32)]
    all_to_all x1 -> x0, local copies, waits for them, and re-layouts: 4.74 us -> none  [per_device(): lax.all_to_all(full_amp, 'pair', split_axis=1, concat_axis=0, tiled=True)]
  transfers between devices with their start and end apart: 2 -> 0, of which waited for: 2 -> 0; matrix products, arithmetic and copies ran while one was open for 0% -> 0% of each run, Pallas kernels for 0% -> 0%
where the time goes in v1:
time: 56.3 us; the launch traced here: 55.4 us
  Pallas kernels  51.5 us (91%)
  local copies, waits for them, and re-layouts  2.99 us (5%)
  between operations  0.7 us (1%)
    pallas_call x1, Pallas kernels, ladder(): pl.pallas_call(functools.partial(kernel, cap, slots), out_shape=(jax.Shap...  51.5 us
    slice x1, local copies, waits for them, and re-layouts, per_device(): fits[0, 0] > 0.0  1.19 us

profile of v1, /device:TPU:2, one launch (start us, length us, event | category | flops | bytes accessed | tf_op | source)
XLA Modules:
  0.0 55.4 jit_solution(17623933625805857573)
XLA Ops:
  0.0 0.0 copy-start.2
  0.0 0.0 copy-start
  0.0 0.0 copy-start.1
  0.0 0.8 %reshape.7.irr_ref = s32[1,384]{1,0:T(1,128)S(1)} reshape(s32[384]{0:T(512)} %param.9) | data formatting | bytes 3072 | tf_op jit(solution)/shard_map/reshape | solution.py:338
  0.8 51.5 %ladder_448.1 = (bf16[384,1280]{1,0:T(8,128)(2,1)S(1)}, f32[8,128]{1,0:T(8,128)}) custom-call(s32[9]{0:T(128)} %start_ref.1, s32[1,384]{1,0:T(1,128)S(1)} %reshape.7.irr_ref, bf16[64,384]{1,0:T(8,128)(2,1)} %bitcast.2, bf16[1024,1280]{1,0:T(8,128)(2,1)} %int_ref.1), custom_call_target="tpu_custom_call" | custom-call | tf_op jit(solution)/shard_map/ladder_448/pallas_call | solution.py:308
  52.3 1.2 %slice.3 = f32[1,1]{1,0:T(1,128)} slice(f32[8,128]{1,0:T(8,128)} %get-tuple-element.24), slice={[0:1], [0:1]} | slice | bytes 8 | tf_op jit(solution)/shard_map/slice | solution.py:341
  54.2 0.0 copy-done.2
  54.2 0.0 copy-done
  54.2 0.0 copy-done.1
  54.2 0.2 conditional.1
  54.4 0.9 %copy.10 = bf16[384,1280]{1,0:T(8,128)(2,1)} copy(bf16[384,1280]{1,0:T(8,128)(2,1)S(1)} %get-tuple-element.26) | data formatting | bytes 1966080
Async XLA Ops:
  0.0 54.2 %copy-start.2 = (s32[9]{0:T(128)S(1)}, s32[9]{0:T(128)}, u32[]{:S(2)}) copy-start(s32[9]{0:T(128)} %start_ref.1) | copy-start | bytes 112
  0.0 54.2 %copy-start = (bf16[1024,1280]{1,0:T(8,128)(2,1)S(1)}, bf16[1024,1280]{1,0:T(8,128)(2,1)}, u32[]{:S(2)}) copy-start(bf16[1024,1280]{1,0:T(8,128)(2,1)} %int_ref.1) | copy-start | bytes 7864324
  0.0 54.2 %copy-start.1 = (bf16[384,64]{0,1:T(8,128)(2,1)S(1)}, bf16[384,64]{0,1:T(8,128)(2,1)}, u32[]{:S(2)}) copy-start(bf16[384,64]{0,1:T(8,128)(2,1)} %param.6) | copy-start | bytes 147460

commit v2 on v1

v2 whole, which is shorter than its diff:
```python
import functools

import jax
import jax.numpy as jnp
from jax import lax
from jax.experimental import pallas as pl
from jax.experimental.pallas import tpu as pltpu
from jax.sharding import PartitionSpec as P

MESH = pl.DeviceIdType.MESH
NX, NZ = 4, 8
TILE = 256
F32 = jnp.float32


def iota(shape, axis):
    return lax.broadcasted_iota(jnp.int32, shape, axis)


def kernel(
    cap, slots,
    start_ref, irr_ref, amp_ref, int_ref,
    out_ref, flag_ref,
    irr_all, comp, gat_a, gat_b, ints, pick, lhs, own, mix, low, acc, sendb, recvb,
    irr_send, irr_recv, a_send, a_recv, b_send, b_recv, z_send, z_recv, x_send, x_recv,
    int_send, int_recv, own_sem, ex_send, ex_recv, ready,
):
    pairs = irr_ref.shape[0]
    depth, cols = int_ref.shape
    rows = amp_ref.shape[0]
    part = rows // 2
    half = 2 * depth
    tiles = cols // TILE

    pair = lax.axis_index("pair")
    col = lax.axis_index("col")
    h, core = pair // 2, pair % 2
    yh, x, z = col // (NX * NZ), (col // NZ) % NX, col % NZ
    kind = (h == yh).astype(jnp.int32)
    selfish = h == yh

    def at(hh, cc, yy, xx, zz):
        return (hh * 2 + cc, (yy * NX + xx) * NZ + zz)

    def xs(d):
        return (x + NX + d) % NX

    def zs(d):
        return (z + NZ + d) % NZ

    def remote(src, dst, send, recv, dev):
        return pltpu.make_async_remote_copy(
            src_ref=src, dst_ref=dst, send_sem=send, recv_sem=recv, device_id=dev, device_id_type=MESH
        )

    sibling = at(h, 1 - core, yh, x, z)
    partner = at(1 - h, core, yh, x, z)

    barrier = pltpu.get_barrier_semaphore()

    def signal(dev):
        pl.semaphore_signal(barrier, inc=1, device_id=dev, device_id_type=MESH)

    near = [at(h, core, yh, x, zs(d)) for d in (1, -1, 2, -2)] + [at(h, core, yh, xs(d), z) for d in (1, -1)]

    @pl.when(core == 0)
    def _():
        signal(sibling)

    signal(partner)
    for dev in near:
        signal(dev)
    for u in range(2):
        for d in range(NX):
            if d:
                signal(at(u, core, h, xs(d), z))
        for d in range(NZ):
            if d:
                signal(at(u, core, h, x, zs(d)))

        @pl.when(jnp.logical_not(jnp.logical_and(selfish, u == h)))
        def _(u=u):
            pl.semaphore_signal(barrier, inc=2, device_id=at(u, core, h, x, z), device_id_type=MESH)

    own_copy = pltpu.make_async_copy(int_ref, ints.at[pl.ds(core * depth, depth)], own_sem)
    own_copy.start()

    def row_irrep(row):
        total = jnp.int32(0)
        for j in range(1, 8):
            total = total + (row >= start_ref[j]).astype(jnp.int32)
        return total

    eye = iota((pairs, pairs), 0) == iota((pairs, pairs), 1)
    below = iota((pairs, pairs), 1) < iota((pairs, pairs), 0)
    above = iota((pairs, pairs), 0) < iota((pairs, pairs), 1)

    def down(v):
        return jnp.sum(jnp.where(eye, v, 0.0), axis=1, keepdims=True)

    def touch(v, which):
        total = jnp.zeros_like(v)
        for r in range(8):
            meets = jnp.logical_and(start_ref[r] < half * (which + 1), start_ref[r + 1] > half * which)
            total = total + jnp.where(v == float(r), jnp.where(meets, 1.0, 0.0), 0.0)
        return total

    mine = irr_ref[...].reshape(1, pairs)
    irr_all[pair] = mine
    mine_l = mine.astype(F32)
    mine_s = down(mine_l)
    rank_s = jnp.sum(jnp.where(jnp.logical_and(below, mine_s == mine_l), 1.0, 0.0), axis=1, keepdims=True)
    here = row_irrep(col * rows).astype(F32)
    where_s = jnp.where(mine_s == here, rank_s, -1.0)
    chosen = jnp.where(where_s == iota((pairs, cap), 1).astype(F32), 1.0, 0.0).astype(jnp.bfloat16)
    block = jnp.dot(amp_ref[...], chosen, preferred_element_type=F32).astype(jnp.bfloat16)
    comp[...] = block

    @pl.when(selfish)
    def _():
        gat_a[1, z, x] = block[:part]
        gat_b[1, x, z] = block[part:]

    pick_own = (mine_s * 512.0 + rank_s).astype(jnp.int32) - iota((pairs, cap), 1)

    pl.semaphore_wait(barrier, 1 + len(near) + 2 * (NX + NZ - kind) + core)

    def a_copy(u, d):
        return remote(
            comp.at[pl.ds(0, part)], gat_a.at[kind, z, x], a_send.at[u * NX + d], a_recv.at[kind, x],
            at(yh, core, u, xs(d), z),
        )

    def b_copy(u, d):
        return remote(
            comp.at[pl.ds(part, part)], gat_b.at[kind, x, z], b_send.at[u * NZ + d], b_recv.at[kind, z],
            at(yh, core, u, x, zs(d)),
        )

    def first_hops(act):
        for d in (4, 3, 5, 2, 6, 1, 7):
            for u in range(2):
                act(b_copy(u, d))
                if d < NX:
                    act(a_copy(u, d))
        for u in range(2):
            @pl.when(jnp.logical_not(jnp.logical_and(selfish, u == yh)))
            def _(u=u):
                act(a_copy(u, 0))
                act(b_copy(u, 0))

    def irr_copy(k):
        g = pair if k < 2 else (1 - h) * 2 + core
        return remote(irr_all.at[g], irr_all.at[g], irr_send.at[k], irr_recv.at[k], partner if k == 0 else sibling)

    def irr_arrival(k):
        g = ((1 - h) * 2 + core, h * 2 + 1 - core, (1 - h) * 2 + 1 - core)[k]
        return remote(irr_all.at[g], irr_all.at[g], irr_send.at[k], irr_recv.at[k], sibling)

    int_copy = remote(int_ref, ints.at[pl.ds(core * depth, depth)], int_send, int_recv, sibling)
    int_arrival = remote(int_ref, ints.at[pl.ds((1 - core) * depth, depth)], int_send, int_recv, sibling)

    irr_copy(0).start()
    first_hops(lambda c: c.start())

    @pl.when(core == 1)
    def _():
        pl.semaphore_signal(ready, inc=1, device_id=sibling, device_id_type=MESH)
        int_copy.start()

    src_l = touch(mine_l, 1 - h)
    both_l = src_l * touch(mine_l, h)
    src_s, both_s = down(src_l), down(both_l)
    pos1 = jnp.sum(jnp.where(below, src_l, 0.0), axis=1, keepdims=True)
    pos2 = jnp.sum(src_l, axis=1, keepdims=True) + jnp.sum(jnp.where(below, both_l, 0.0), axis=1, keepdims=True)
    pos1 = jnp.where(src_s > 0.0, pos1, -1.0)
    pos2 = jnp.where(both_s > 0.0, pos2, -1.0)
    slot = iota((pairs, slots), 1).astype(F32)
    mix[...] = jnp.where(jnp.logical_or(pos1 == slot, pos2 == slot), 1.0, 0.0).astype(jnp.bfloat16)

    irr_arrival(0).wait_recv()
    theirs_l = irr_all[(1 - h) * 2 + core].astype(F32)
    theirs_s = down(theirs_l)
    rank_l = jnp.sum(jnp.where(jnp.logical_and(above, theirs_s == theirs_l), 1.0, 0.0), axis=0, keepdims=True)
    key_l = theirs_l * 512.0 + rank_l + 1.0
    src_l = touch(theirs_l, h)
    both_l = src_l * touch(theirs_l, 1 - h)
    src_s, both_s = down(src_l), down(both_l)
    pos1 = jnp.sum(jnp.where(above, src_s, 0.0), axis=0, keepdims=True)
    pos2 = jnp.sum(src_l, axis=1, keepdims=True) + jnp.sum(jnp.where(above, both_s, 0.0), axis=0, keepdims=True)
    pos1 = jnp.where(src_l > 0.0, pos1, -1.0)
    pos2 = jnp.where(both_l > 0.0, pos2, -1.0)
    slot = iota((slots, pairs), 0).astype(F32)
    is_low = pos2 == slot
    key_slot = jnp.sum(jnp.where(jnp.logical_or(pos1 == slot, is_low), key_l, 0.0), axis=1, keepdims=True)
    low[...] = jnp.sum(jnp.where(is_low, 1.0, 0.0), axis=1, keepdims=True)
    pick[...] = (key_slot - 1.0).astype(jnp.int32) - iota((slots, cap), 1)

    def z_ref(t, d, piece):
        ref = gat_a.at[t, zs(d)]
        return ref if piece is None else ref.at[pl.ds(piece * (NX // 2), NX // 2)]

    z_plan = (
        (0, 2, None), (0, -2, None), (0, 1, None), (0, -1, None),
        (-2, 1, None), (2, -1, None), (-2, 2, 0), (2, -2, 1),
    )

    def z_copy(t, i):
        d, to, piece = z_plan[i]
        ref = z_ref(t, d, piece)
        return remote(ref, ref, z_send.at[t, i], z_recv.at[t, i], at(h, core, yh, x, zs(to)))

    def z_arrival(t, i):
        d, to, piece = z_plan[i]
        ref = z_ref(t, d - to, piece)
        return remote(ref, ref, z_send.at[t, i], z_recv.at[t, i], at(h, core, yh, x, zs(to)))

    def x_ref(t, d, piece):
        ref = gat_b.at[t, xs(d)]
        return ref if piece is None else ref.at[pl.ds(piece * (NZ // 2), NZ // 2)]

    x_plan = ((0, 1, None), (0, -1, None), (-1, 1, 0), (1, -1, 1))

    def x_copy(t, i):
        d, to, piece = x_plan[i]
        ref = x_ref(t, d, piece)
        return remote(ref, ref, x_send.at[t, i], x_recv.at[t, i], at(h, core, yh, xs(to), z))

    def x_arrival(t, i):
        d, to, piece = x_plan[i]
        ref = x_ref(t, d - to, piece)
        return remote(ref, ref, x_send.at[t, i], x_recv.at[t, i], at(h, core, yh, xs(to), z))

    def unless_own(t, d, act):
        if t == 1 and d == 0:
            @pl.when(jnp.logical_not(selfish))
            def _():
                act()
        else:
            act()

    def gather_start(t):
        for d in range(NX):
            arrival = remote(comp.at[pl.ds(0, part)], gat_a.at[t, z, xs(d)], a_send.at[0], a_recv.at[t, xs(d)], partner)
            unless_own(t, d, arrival.wait_recv)
        for i in range(4):
            z_copy(t, i).start()
        for d in range(NZ):
            arrival = remote(comp.at[pl.ds(part, part)], gat_b.at[t, x, zs(d)], b_send.at[0], b_recv.at[t, zs(d)], partner)
            unless_own(t, d, arrival.wait_recv)
        for i in range(2):
            x_copy(t, i).start()

    def gather_rest(t):
        z_arrival(t, 0).wait_recv()
        z_copy(t, 4).start()
        z_copy(t, 6).start()
        z_arrival(t, 1).wait_recv()
        z_copy(t, 5).start()
        z_copy(t, 7).start()
        for i in range(2):
            x_arrival(t, i).wait_recv()
            x_copy(t, 2 + i).start()
        for i in range(2, 8):
            z_arrival(t, i).wait_recv()
        for i in range(2, 4):
            x_arrival(t, i).wait_recv()

    gather_start(0)

    @pl.when(core == 0)
    def _():
        pl.semaphore_wait(ready, 1)
        int_copy.start()

    irr_copy(1).start()
    irr_copy(2).start()

    gather_rest(0)

    def expand(t, keys, dst):
        for b in range(half // 128):
            here = row_irrep(h * half + b * 128) * 512
            one_hot = jnp.where(keys == here, 1.0, 0.0).astype(jnp.bfloat16)
            zz, xx = 2 * (b % (NZ // 2)), b // (NZ // 2)
            packed = jnp.concatenate(
                [gat_a[t, zz, xx], gat_b[t, xx, zz], gat_a[t, zz + 1, xx], gat_b[t, xx, zz + 1]], axis=0
            )
            full = lax.dot_general(one_hot, packed, (((1,), (1,)), ((), ())), preferred_element_type=F32)
            dst[:, pl.ds(b * 128, 128)] = full.astype(jnp.bfloat16)

    expand(0, pick[...], lhs)
    own_copy.wait()
    int_arrival.wait_recv()

    def ex_copy(j):
        return remote(sendb.at[j], recvb.at[j], ex_send.at[j], ex_recv.at[j], partner)

    @pl.loop(0, tiles + 1)
    def _(j):
        @pl.when(j < tiles)
        def _():
            full = jnp.dot(lhs[...], ints[:, pl.ds(pl.multiple_of(j * TILE, TILE), TILE)], preferred_element_type=F32)
            high = full.astype(jnp.bfloat16).astype(F32)
            sendb[j] = jnp.where(low[...] > 0.0, full - high, full).astype(jnp.bfloat16)

        @pl.when(j > 0)
        def _():
            ex_copy(j - 1).start()

    gather_start(1)
    irr_arrival(1).wait_recv()
    irr_arrival(2).wait_recv()
    fits = jnp.ones((1, 1), F32)
    for g in range(4):
        v = irr_all[g].astype(F32)
        for r in range(8):
            count = jnp.sum(jnp.where(v == float(r), 1.0, 0.0), axis=1, keepdims=True)
            fits = jnp.where(count > float(cap), 0.0, fits)
        src = touch(v, 1 - g // 2)
        need = jnp.sum(src + src * touch(v, g // 2), axis=1, keepdims=True)
        fits = jnp.where(need > float(slots), 0.0, fits)
    flag_ref[0] = jnp.sum(fits).astype(jnp.int32)

    gather_rest(1)
    expand(1, pick_own, own)

    @pl.loop(0, tiles)
    def _(j):
        acc[j] = jnp.dot(own[...], ints[:, pl.ds(pl.multiple_of(j * TILE, TILE), TILE)], preferred_element_type=F32)

    @pl.loop(0, tiles)
    def _(j):
        ex_copy(j).wait_recv()
        total = acc[j] + jnp.dot(mix[...], recvb[j], preferred_element_type=F32)
        out_ref[:, pl.ds(pl.multiple_of(j * TILE, TILE), TILE)] = total.astype(jnp.bfloat16)

    first_hops(lambda c: c.wait_send())
    for k in range(3):
        irr_copy(k).wait_send()
    int_copy.wait_send()
    for t in range(2):
        for i in range(8):
            z_copy(t, i).wait_send()
        for i in range(4):
            x_copy(t, i).wait_send()

    @pl.loop(0, tiles)
    def _(j):
        ex_copy(j).wait_send()


def ladder(cap, slots, collective_id, starts, irreps, amp, integrals):
    rows, pairs = amp.shape
    depth, cols = integrals.shape
    half, tiles = 2 * depth, cols // TILE
    bf16 = jnp.bfloat16
    dma = pltpu.SemaphoreType.DMA
    vmem = pl.BlockSpec(memory_space=pltpu.VMEM)
    return pl.pallas_call(
        functools.partial(kernel, cap, slots),
        out_shape=(jax.ShapeDtypeStruct((pairs, cols), bf16), jax.ShapeDtypeStruct((1,), jnp.int32)),
        in_specs=[pl.BlockSpec(memory_space=pltpu.SMEM), vmem, vmem, pl.BlockSpec(memory_space=pl.ANY)],
        out_specs=(vmem, pl.BlockSpec(memory_space=pltpu.SMEM)),
        scratch_shapes=[
            pltpu.VMEM((4, 1, pairs), jnp.int32),
            pltpu.VMEM((rows, cap), bf16),
            pltpu.VMEM((2, NZ, NX, rows // 2, cap), bf16),
            pltpu.VMEM((2, NX, NZ, rows // 2, cap), bf16),
            pltpu.VMEM((half, cols), bf16),
            pltpu.VMEM((slots, cap), jnp.int32),
            pltpu.VMEM((slots, half), bf16),
            pltpu.VMEM((pairs, half), bf16),
            pltpu.VMEM((pairs, slots), bf16),
            pltpu.VMEM((slots, 1), F32),
            pltpu.VMEM((tiles, pairs, TILE), F32),
            pltpu.VMEM((tiles, slots, TILE), bf16),
            pltpu.VMEM((tiles, slots, TILE), bf16),
            dma((3,)), dma((3,)), dma((2 * NX,)), dma((2, NX)), dma((2 * NZ,)), dma((2, NZ)),
            dma((2, 8)), dma((2, 8)), dma((2, 4)), dma((2, 4)),
            dma, dma, dma, dma((tiles,)), dma((tiles,)), pltpu.SemaphoreType.REGULAR,
        ],
        compiler_params=pltpu.CompilerParams(
            collective_id=collective_id, has_side_effects=True, vmem_limit_bytes=56 * 1024 * 1024
        ),
        name="ladder_" + str(slots),
    )(starts, irreps, amp, integrals)


def per_device(amplitudes, integrals, irrep_start, pair_irrep):
    pairs = amplitudes.shape[0]
    operands = (irrep_start, pair_irrep, amplitudes.T, integrals)
    out, fits = ladder(128, 448, 0, *operands)
    return lax.cond(
        fits[0] > 0,
        lambda *_: out,
        lambda *args: ladder(pairs, 2 * pairs, 1, *args)[0],
        *operands,
    )


def solution(mesh):
    placed = (P("pair", "col"), P("pair", "col"), P(), P("pair"))
    return jax.shard_map(
        per_device, mesh=mesh, in_specs=placed, out_specs=P("pair", "col"), check_vma=False
    )
```

time: 56.3 us -> 53.1 us (0.943); the launches traced: 55.4 us -> 53 us
  local copies, waits for them, and re-layouts: 2.99 us -> 0.96 us
    slice x1 -> x0, local copies, waits for them, and re-layouts: 1.19 us -> none  [per_device(): fits[0, 0] > 0.0]
    reshape x1 -> x0, local copies, waits for them, and re-layouts: 0.83 us -> none  [per_device(): pair_irrep.reshape(1, pairs)]
where the time goes in v2:
time: 53.1 us; the launch traced here: 53 us
  Pallas kernels  51.2 us (96%)
  local copies, waits for them, and re-layouts  0.96 us (2%)
  between operations  0.62 us (1%)
    pallas_call x1, Pallas kernels, ladder(): pl.pallas_call(functools.partial(kernel, cap, slots), out_shape=(jax.Shap...  51.2 us

profile of v2, /device:TPU:2, one launch (start us, length us, event | category | flops | bytes accessed | tf_op | source)
XLA Modules:
  0.0 53.0 jit_solution(17004314182208106412)
XLA Ops:
  0.0 0.0 copy-start.2
  0.0 0.0 copy-start.3
  0.0 0.0 copy-start
  0.0 0.0 copy-start.1
  0.0 51.2 %ladder_448.1 = (bf16[384,1280]{1,0:T(8,128)(2,1)S(1)}, s32[1]{0:T(128)}) custom-call(s32[9]{0:T(128)} %start_ref.1, s32[384]{0:T(512)} %irr_ref.1, bf16[64,384]{1,0:T(8,128)(2,1)} %bitcast.2, bf16[1024,1280]{1,0:T(8,128)(2,1)} %int_ref.1), custom_call_target="tpu_custom_call" | custom-call | tf_op jit(solution)/shard_map/ladder_448/pallas_call | solution.py:360
  51.8 0.0 copy-done.2
  51.8 0.0 copy-done.3
  51.8 0.0 copy-done
  51.8 0.0 copy-done.1
  51.8 0.2 conditional.1
  52.1 0.9 %copy.10 = bf16[384,1280]{1,0:T(8,128)(2,1)} copy(bf16[384,1280]{1,0:T(8,128)(2,1)S(1)} %get-tuple-element.26) | data formatting | bytes 1966080
Async XLA Ops:
  0.0 51.8 %copy-start.2 = (s32[384]{0:T(512)S(1)}, s32[384]{0:T(512)}, u32[]{:S(2)}) copy-start(s32[384]{0:T(512)} %irr_ref.1) | copy-start | bytes 4612
  0.0 51.8 %copy-start.3 = (s32[9]{0:T(128)S(1)}, s32[9]{0:T(128)}, u32[]{:S(2)}) copy-start(s32[9]{0:T(128)} %start_ref.1) | copy-start | bytes 112
  0.0 51.8 %copy-start = (bf16[1024,1280]{1,0:T(8,128)(2,1)S(1)}, bf16[1024,1280]{1,0:T(8,128)(2,1)}, u32[]{:S(2)}) copy-start(bf16[1024,1280]{1,0:T(8,128)(2,1)} %int_ref.1) | copy-start | bytes 7864324
  0.0 51.8 %copy-start.1 = (bf16[384,64]{0,1:T(8,128)(2,1)S(1)}, bf16[384,64]{0,1:T(8,128)(2,1)}, u32[]{:S(2)}) copy-start(bf16[384,64]{0,1:T(8,128)(2,1)} %param.6) | copy-start | bytes 147460

commit v3 on v0

v3 whole, which is shorter than its diff:
```python
import functools

import jax
import jax.numpy as jnp
from jax import lax
from jax.experimental import pallas as pl
from jax.experimental.pallas import tpu as pltpu
from jax.sharding import PartitionSpec as P

MESH = pl.DeviceIdType.MESH
NX, NZ = 4, 8
TILE = 256
F32 = jnp.float32


def iota(shape, axis):
    return lax.broadcasted_iota(jnp.int32, shape, axis)


PART = 16
SIZES = (256, 304, 352, 448)
CAP = 128


class Place:
    def __init__(self):
        pair, col = lax.axis_index("pair"), lax.axis_index("col")
        self.pair, self.col = pair, col
        self.h, self.core = pair // 2, pair % 2
        self.yh, self.x, self.z = col // (NX * NZ), (col // NZ) % NX, col % NZ
        self.group = (1 - self.h) * 2 + self.core
        self.partner = self.at(1 - self.h, self.core, self.yh, self.x, self.z)
        self.sibling = self.at(self.h, 1 - self.core, self.yh, self.x, self.z)
        self.near = [self.along_z(d) for d in (1, -1, 2, -2)] + [self.along_x(d) for d in (1, -1)]

    def at(self, h, core, yh, x, z):
        return (h * 2 + core, (yh * NX + x) * NZ + z)

    def xs(self, d):
        return (self.x + NX + d) % NX

    def zs(self, d):
        return (self.z + NZ + d) % NZ

    def along_z(self, d):
        return self.at(self.h, self.core, self.yh, self.x, self.zs(d))

    def along_x(self, d):
        return self.at(self.h, self.core, self.yh, self.xs(d), self.z)


def remote(src, dst, send, recv, dev):
    return pltpu.make_async_remote_copy(
        src_ref=src, dst_ref=dst, send_sem=send, recv_sem=recv, device_id=dev, device_id_type=MESH
    )


def row_irrep(start_ref, row):
    total = jnp.int32(0)
    for j in range(1, 8):
        total = total + (row >= start_ref[j]).astype(jnp.int32)
    return total


def touch(start_ref, v, which, half):
    total = jnp.zeros_like(v)
    for r in range(8):
        meets = jnp.logical_and(start_ref[r] < half * (which + 1), start_ref[r + 1] > half * which)
        total = total + jnp.where(v == float(r), jnp.where(meets, 1.0, 0.0), 0.0)
    return total


def down(v):
    n = v.shape[1]
    return jnp.sum(jnp.where(iota((n, n), 0) == iota((n, n), 1), v, 0.0), axis=1, keepdims=True)


def expand(start_ref, first_row, half, keys, slab, column, dst):
    for b in range(half // 128):
        here = row_irrep(start_ref, first_row + b * 128) * 512
        one_hot = jnp.where(keys == here, 1.0, 0.0).astype(jnp.bfloat16)
        zz, xx = 2 * (b % (NZ // 2)), b // (NZ // 2)
        packed = jnp.concatenate([slab(zz, xx), column(xx, zz), slab(zz + 1, xx), column(xx, zz + 1)], axis=0)
        full = lax.dot_general(one_hot, packed, (((1,), (1,)), ((), ())), preferred_element_type=F32)
        dst[:, pl.ds(b * 128, 128)] = full.astype(jnp.bfloat16)


Z_PLAN = (
    (0, 2, None), (0, -2, None), (0, 1, None), (0, -1, None),
    (-2, 1, None), (2, -1, None), (-2, 2, 0), (2, -2, 1),
)
X_PLAN = ((0, 1, None), (0, -1, None), (-1, 1, 0), (1, -1, 1))


def hop(place, axis, i, src, dst, send, recv, arriving=False):
    d, to, piece = (Z_PLAN if axis == "z" else X_PLAN)[i]
    index = place.zs if axis == "z" else place.xs
    n = (NX if axis == "z" else NZ) // 2

    def view(ref):
        ref = ref.at[index(d - to if arriving else d)]
        return ref if piece is None else ref.at[pl.ds(piece * n, n)]

    return remote(view(src), view(dst), send, recv, place.along_z(to) if axis == "z" else place.along_x(to))


def first_kernel(
    cap, slots,
    start_ref, irr_ref, amp_ref, int_ref,
    lhs, low, ints, gat_a, gat_b, irr_all, size_ref,
    comp,
    irr_send, irr_recv, a_send, a_recv, b_send, b_recv, z_send, z_recv, x_send, x_recv,
    int_send, int_recv, own_sem, ready,
):
    p = Place()
    pairs = irr_ref.shape[0]
    depth, cols = int_ref.shape
    rows = amp_ref.shape[0]
    half = 2 * depth
    kind = (p.h == p.yh).astype(jnp.int32)
    selfish = p.h == p.yh

    barrier = pltpu.get_barrier_semaphore()

    def signal(dev, inc=1):
        pl.semaphore_signal(barrier, inc=inc, device_id=dev, device_id_type=MESH)

    @pl.when(p.core == 0)
    def _():
        signal(p.sibling)

    signal(p.partner)
    for dev in p.near:
        signal(dev)
    for u in range(2):
        for d in range(1, NX):
            signal(p.at(u, p.core, p.h, p.xs(d), p.z))
        for d in range(1, NZ):
            signal(p.at(u, p.core, p.h, p.x, p.zs(d)))

        @pl.when(jnp.logical_not(jnp.logical_and(selfish, u == p.h)))
        def _(u=u):
            signal(p.at(u, p.core, p.h, p.x, p.z), 2)

    own_copy = pltpu.make_async_copy(int_ref, ints.at[pl.ds(p.core * depth, depth)], own_sem)
    own_copy.start()

    mine = irr_ref[...].reshape(1, pairs)
    irr_all[p.pair] = mine
    mine_l = mine.astype(F32)
    mine_s = down(mine_l)
    below = iota((pairs, pairs), 1) < iota((pairs, pairs), 0)
    rank_s = jnp.sum(jnp.where(jnp.logical_and(below, mine_s == mine_l), 1.0, 0.0), axis=1, keepdims=True)
    here = row_irrep(start_ref, p.col * rows).astype(F32)
    where_s = jnp.where(mine_s == here, rank_s, -1.0)
    chosen = jnp.where(where_s == iota((pairs, cap), 1).astype(F32), 1.0, 0.0).astype(jnp.bfloat16)
    block = jnp.dot(amp_ref[...], chosen, preferred_element_type=F32).astype(jnp.bfloat16)
    comp[...] = block

    @pl.when(selfish)
    def _():
        gat_a[1, p.z, p.x] = block[:PART]
        gat_b[1, p.x, p.z] = block[PART:]

    pl.semaphore_wait(barrier, 1 + len(p.near) + 2 * (NX + NZ - kind) + p.core)

    comp_a, comp_b = comp.at[pl.ds(0, PART)], comp.at[pl.ds(PART, rows - PART)]

    def a_copy(u, d):
        dev = p.at(p.yh, p.core, u, p.xs(d), p.z)
        return remote(comp_a, gat_a.at[kind, p.z, p.x], a_send.at[u * NX + d], a_recv.at[kind, p.x], dev)

    def b_copy(u, d):
        dev = p.at(p.yh, p.core, u, p.x, p.zs(d))
        return remote(comp_b, gat_b.at[kind, p.x, p.z], b_send.at[u * NZ + d], b_recv.at[kind, p.z], dev)

    def first_hops(act):
        for d in (4, 3, 5, 2, 6, 1, 7):
            for u in range(2):
                act(b_copy(u, d))
                if d < NX:
                    act(a_copy(u, d))
        for u in range(2):
            @pl.when(jnp.logical_not(jnp.logical_and(selfish, u == p.yh)))
            def _(u=u):
                act(a_copy(u, 0))
                act(b_copy(u, 0))

    def irr_copy(k):
        g = p.pair if k < 2 else p.group
        dev = p.partner if k == 0 else p.sibling
        return remote(irr_all.at[g], irr_all.at[g], irr_send.at[k], irr_recv.at[k], dev)

    def irr_arrival(k):
        g = (p.group, p.h * 2 + 1 - p.core, (1 - p.h) * 2 + 1 - p.core)[k]
        return remote(irr_all.at[g], irr_all.at[g], irr_send.at[k], irr_recv.at[k], p.sibling)

    int_copy = remote(int_ref, ints.at[pl.ds(p.core * depth, depth)], int_send, int_recv, p.sibling)
    int_arrival = remote(int_ref, ints.at[pl.ds((1 - p.core) * depth, depth)], int_send, int_recv, p.sibling)

    irr_copy(0).start()
    first_hops(lambda c: c.start())

    @pl.when(p.core == 1)
    def _():
        pl.semaphore_signal(ready, inc=1, device_id=p.sibling, device_id_type=MESH)

    @pl.when(p.core == 0)
    def _():
        pl.semaphore_wait(ready, 1)

    int_copy.start()
    irr_copy(1).start()

    irr_arrival(0).wait_recv()
    irr_copy(2).start()
    theirs_l = irr_all[p.group].astype(F32)
    theirs_s = down(theirs_l)
    above = iota((pairs, pairs), 0) < iota((pairs, pairs), 1)
    rank_l = jnp.sum(jnp.where(jnp.logical_and(above, theirs_s == theirs_l), 1.0, 0.0), axis=0, keepdims=True)
    key_l = theirs_l * 512.0 + rank_l + 1.0
    src_l = touch(start_ref, theirs_l, p.h, half)
    both_l = src_l * touch(start_ref, theirs_l, 1 - p.h, half)
    src_s, both_s = down(src_l), down(both_l)
    pos1 = jnp.sum(jnp.where(above, src_s, 0.0), axis=0, keepdims=True)
    pos2 = jnp.sum(src_l, axis=1, keepdims=True) + jnp.sum(jnp.where(above, both_s, 0.0), axis=0, keepdims=True)
    pos1 = jnp.where(src_l > 0.0, pos1, -1.0)
    pos2 = jnp.where(both_l > 0.0, pos2, -1.0)
    slot = iota((slots, pairs), 0).astype(F32)
    is_low = pos2 == slot
    key_slot = jnp.sum(jnp.where(jnp.logical_or(pos1 == slot, is_low), key_l, 0.0), axis=1, keepdims=True)
    low[...] = jnp.sum(jnp.where(is_low, 1.0, 0.0), axis=1, keepdims=True)
    pick = (key_slot - 1.0).astype(jnp.int32) - iota((slots, cap), 1)

    def z_hop(t, i, arriving=False):
        return hop(p, "z", i, gat_a.at[t], gat_a.at[t], z_send.at[t, i], z_recv.at[t, i], arriving)

    def x_hop(t, i, arriving=False):
        return hop(p, "x", i, gat_b.at[t], gat_b.at[t], x_send.at[t, i], x_recv.at[t, i], arriving)

    def unless_own(t, d, act):
        if t == 1 and d == 0:
            @pl.when(jnp.logical_not(selfish))
            def _():
                act()
        else:
            act()

    def gather_start(t):
        for d in range(NZ):
            arrival = remote(comp_b, gat_b.at[t, p.x, p.zs(d)], b_send.at[0], b_recv.at[t, p.zs(d)], p.partner)
            unless_own(t, d, arrival.wait_recv)
        for i in range(2):
            x_hop(t, i).start()
        for d in range(NX):
            arrival = remote(comp_a, gat_a.at[t, p.z, p.xs(d)], a_send.at[0], a_recv.at[t, p.xs(d)], p.partner)
            unless_own(t, d, arrival.wait_recv)
        for i in range(4):
            z_hop(t, i).start()

    gather_start(0)
    for i in range(2):
        x_hop(0, i, True).wait_recv()
        x_hop(0, 2 + i).start()
    for i in range(2):
        z_hop(0, i, True).wait_recv()
        z_hop(0, 4 + i).start()
        z_hop(0, 6 + i).start()
    gather_start(1)

    irr_arrival(1).wait_recv()
    irr_arrival(2).wait_recv()
    most = jnp.zeros((1, 1), F32)
    for g in range(4):
        v = irr_all[g].astype(F32)
        for r in range(8):
            count = jnp.sum(jnp.where(v == float(r), 1.0, 0.0), axis=1, keepdims=True)
            most = jnp.where(count > float(cap), 1e6, most)
        src = touch(start_ref, v, 1 - g // 2, half)
        need = jnp.sum(src + src * touch(start_ref, v, g // 2, half), axis=1, keepdims=True)
        most = jnp.maximum(most, need)
    choice = jnp.zeros((1, 1), F32)
    for size in SIZES:
        choice = choice + jnp.where(most <= float(size), 1.0, 0.0)
    size_ref[0] = jnp.sum(choice).astype(jnp.int32)

    for i in range(2, 4):
        x_hop(0, i, True).wait_recv()
    for i in range(2, 8):
        z_hop(0, i, True).wait_recv()
    expand(
        start_ref, p.h * half, half, pick,
        lambda zz, xx: gat_a[0, zz, xx], lambda xx, zz: gat_b[0, xx, zz], lhs,
    )
    for i in range(2):
        x_hop(1, i, True).wait_recv()
    for i in range(4):
        z_hop(1, i, True).wait_recv()
    own_copy.wait()
    int_arrival.wait_recv()

    first_hops(lambda c: c.wait_send())
    for k in range(3):
        irr_copy(k).wait_send()
    int_copy.wait_send()
    for t in range(2):
        for i in range(4 if t else 8):
            z_hop(t, i).wait_send()
        for i in range(2 if t else 4):
            x_hop(t, i).wait_send()


def second_kernel(
    cap, slots,
    start_ref, lhs, low, ints, gat_a, gat_b, irr_all,
    out_ref,
    slabs, columns, own, mix, acc, sendb, recvb,
    z_send, z_recv, x_send, x_recv, ex_send, ex_recv,
):
    p = Place()
    pairs = irr_all.shape[2]
    half, cols = ints.shape
    tiles = cols // TILE

    barrier = pltpu.get_barrier_semaphore()
    for dev in p.near + [p.partner]:
        pl.semaphore_signal(barrier, inc=1, device_id=dev, device_id_type=MESH)

    def span(j):
        return pl.ds(pl.multiple_of(j * TILE, TILE), TILE)

    def product(j):
        full = jnp.dot(lhs[pl.ds(0, slots), :], ints[:, span(j)], preferred_element_type=F32)
        high = full.astype(jnp.bfloat16).astype(F32)
        sendb[j] = jnp.where(low[pl.ds(0, slots), :] > 0.0, full - high, full).astype(jnp.bfloat16)

    def ex_copy(j):
        return remote(sendb.at[j], recvb.at[j], ex_send.at[j], ex_recv.at[j], p.partner)

    product(0)
    pl.semaphore_wait(barrier, len(p.near) + 1)

    def z_hop(i, arriving=False):
        return hop(p, "z", i, gat_a.at[1], slabs, z_send.at[i - 4], z_recv.at[i - 4], arriving)

    def x_hop(i, arriving=False):
        return hop(p, "x", i, gat_b.at[1], columns, x_send.at[i - 2], x_recv.at[i - 2], arriving)

    for i in range(2, 4):
        x_hop(i).start()
    for i in range(4, 8):
        z_hop(i).start()

    @pl.loop(1, tiles)
    def _(j):
        product(j)
        ex_copy(j - 1).start()

    mine_l = irr_all[p.pair].astype(F32)
    mine_s = down(mine_l)
    below = iota((pairs, pairs), 1) < iota((pairs, pairs), 0)
    rank_s = jnp.sum(jnp.where(jnp.logical_and(below, mine_s == mine_l), 1.0, 0.0), axis=1, keepdims=True)
    ex_copy(tiles - 1).start()
    src_l = touch(start_ref, mine_l, 1 - p.h, half)
    both_l = src_l * touch(start_ref, mine_l, p.h, half)
    src_s, both_s = down(src_l), down(both_l)
    pos1 = jnp.sum(jnp.where(below, src_l, 0.0), axis=1, keepdims=True)
    pos2 = jnp.sum(src_l, axis=1, keepdims=True) + jnp.sum(jnp.where(below, both_l, 0.0), axis=1, keepdims=True)
    pos1 = jnp.where(src_s > 0.0, pos1, -1.0)
    pos2 = jnp.where(both_s > 0.0, pos2, -1.0)
    slot = iota((pairs, slots), 1).astype(F32)
    mix[...] = jnp.where(jnp.logical_or(pos1 == slot, pos2 == slot), 1.0, 0.0).astype(jnp.bfloat16)
    pick = (mine_s * 512.0 + rank_s).astype(jnp.int32) - iota((pairs, cap), 1)

    for d in range(-2, 3):
        slabs[p.zs(d)] = gat_a[1, p.zs(d)]
    for d in range(-1, 2):
        columns[p.xs(d)] = gat_b[1, p.xs(d)]
    for i in range(2, 4):
        x_hop(i, True).wait_recv()
    for i in range(4, 8):
        z_hop(i, True).wait_recv()
    expand(start_ref, p.h * half, half, pick, lambda zz, xx: slabs[zz, xx], lambda xx, zz: columns[xx, zz], own)

    @pl.loop(0, tiles)
    def _(j):
        acc[j] = jnp.dot(own[...], ints[:, span(j)], preferred_element_type=F32)

    @pl.loop(0, tiles)
    def _(j):
        ex_copy(j).wait_recv()
        total = acc[j] + jnp.dot(mix[...], recvb[j], preferred_element_type=F32)
        out_ref[:, span(j)] = total.astype(jnp.bfloat16)

    for i in range(2, 4):
        x_hop(i).wait_send()
    for i in range(4, 8):
        z_hop(i).wait_send()

    @pl.loop(0, tiles)
    def _(j):
        ex_copy(j).wait_send()


DMA = pltpu.SemaphoreType.DMA
VMEM_SPEC = pl.BlockSpec(memory_space=pltpu.VMEM)
SMEM_SPEC = pl.BlockSpec(memory_space=pltpu.SMEM)


def params(collective_id):
    return pltpu.CompilerParams(
        collective_id=collective_id, has_side_effects=True, vmem_limit_bytes=32 * 1024 * 1024
    )


def first(cap, slots, collective_id, starts, irreps, amp, integrals):
    rows, pairs = amp.shape
    depth, cols = integrals.shape
    bf16 = jnp.bfloat16
    shape = jax.ShapeDtypeStruct
    return pl.pallas_call(
        functools.partial(first_kernel, cap, slots),
        out_shape=(
            shape((slots, 2 * depth), bf16), shape((slots, 1), F32), shape((2 * depth, cols), bf16),
            shape((2, NZ, NX, PART, cap), bf16), shape((2, NX, NZ, rows - PART, cap), bf16),
            shape((4, 1, pairs), jnp.int32), shape((1,), jnp.int32),
        ),
        in_specs=[SMEM_SPEC, VMEM_SPEC, VMEM_SPEC, pl.BlockSpec(memory_space=pl.ANY)],
        out_specs=(VMEM_SPEC,) * 6 + (SMEM_SPEC,),
        scratch_shapes=[
            pltpu.VMEM((rows, cap), bf16),
            DMA((3,)), DMA((3,)), DMA((2 * NX,)), DMA((2, NX)), DMA((2 * NZ,)), DMA((2, NZ)),
            DMA((2, 8)), DMA((2, 8)), DMA((2, 4)), DMA((2, 4)),
            DMA, DMA, DMA, pltpu.SemaphoreType.REGULAR,
        ],
        compiler_params=params(collective_id),
        name="gather_" + str(slots),
    )(starts, irreps, amp, integrals)


def second(cap, slots, collective_id, starts, lhs, low, ints, gat_a, gat_b, irr_all):
    pairs, cols, half = irr_all.shape[2], ints.shape[1], ints.shape[0]
    tiles = cols // TILE
    bf16 = jnp.bfloat16
    return pl.pallas_call(
        functools.partial(second_kernel, cap, slots),
        out_shape=jax.ShapeDtypeStruct((pairs, cols), bf16),
        in_specs=[SMEM_SPEC] + [VMEM_SPEC] * 6,
        out_specs=VMEM_SPEC,
        scratch_shapes=[
            pltpu.VMEM(gat_a.shape[1:], bf16),
            pltpu.VMEM(gat_b.shape[1:], bf16),
            pltpu.VMEM((pairs, half), bf16),
            pltpu.VMEM((pairs, slots), bf16),
            pltpu.VMEM((tiles, pairs, TILE), F32),
            pltpu.VMEM((tiles, slots, TILE), bf16),
            pltpu.VMEM((tiles, slots, TILE), bf16),
            DMA((4,)), DMA((4,)), DMA((2,)), DMA((2,)), DMA((tiles,)), DMA((tiles,)),
        ],
        compiler_params=params(collective_id),
        name="exchange_" + str(slots),
    )(starts, lhs, low, ints, gat_a, gat_b, irr_all)


def per_device(amplitudes, integrals, irrep_start, pair_irrep):
    pairs = amplitudes.shape[0]
    operands = (irrep_start, pair_irrep, amplitudes.T, integrals)
    *state, size = first(CAP, SIZES[-1], 0, *operands)

    def full(state, operands):
        *state, _ = first(pairs, 2 * pairs, 1, *operands)
        return second(pairs, 2 * pairs, 2, operands[0], *state)

    def sized(slots, collective_id):
        return lambda state, operands: second(CAP, slots, collective_id, operands[0], *state)

    branches = [full] + [sized(slots, 3 + i) for i, slots in enumerate(reversed(SIZES))]
    return lax.switch(size[0], branches, state, operands)


def solution(mesh):
    placed = (P("pair", "col"), P("pair", "col"), P(), P("pair"))
    return jax.shard_map(
        per_device, mesh=mesh, in_specs=placed, out_specs=P("pair", "col"), check_vma=False
    )
```

time: 278 us -> 50.9 us (0.18)
  waiting for transfers between devices: 202 us -> 0 us
  Pallas kernels: 0 us -> 48.4 us
  blocking collectives: 42.2 us -> 0 us
  between operations: 13.4 us -> 0.64 us
  matrix products: 9.23 us -> 0 us
  local copies, waits for them, and re-layouts: 5.62 us -> 0.95 us
  other arithmetic: 4.18 us -> 0 us
    all_gather x1 -> x0, waiting for transfers between devices: 128 us -> none  [per_device(): full_amp = lax.all_gather(masked, 'col', axis=1, tiled=True)]
    reduce_scatter x1 -> x0, waiting for transfers between devices: 74 us -> none  [per_device(): lax.psum_scatter(jnp.dot(blocks, integrals, preferred_element_type=jnp.fl...]
    pallas_call x0 -> x2, Pallas kernels: none -> 48.4 us  [the longest x1 27.1 us: first(): pl.pallas_call(functools.partial(first_kernel, cap, slots), out_shape=(sh...]
    all_to_all x1 -> x0, blocking collectives: 42.2 us -> none  [per_device(): lax.all_to_all(full_amp, 'pair', split_axis=1, concat_axis=0, tiled=True)]
    dot_general x1 -> x0, matrix products: 9.23 us -> none  [per_device(): jnp.dot(blocks, integrals, preferred_element_type=jnp.float32)]
    all_to_all x1 -> x0, local copies, waits for them, and re-layouts: 4.74 us -> none  [per_device(): lax.all_to_all(full_amp, 'pair', split_axis=1, concat_axis=0, tiled=True)]
  transfers between devices with their start and end apart: 2 -> 0, of which waited for: 2 -> 0; matrix products, arithmetic and copies ran while one was open for 0% -> 0% of each run, Pallas kernels for 0% -> 0%
where the time goes in v3:
time: 50.9 us; the launch traced here: 50.2 us
  Pallas kernels  48.4 us (95%)
  local copies, waits for them, and re-layouts  0.95 us (2%)
  between operations  0.64 us (1%)
    pallas_call x1, Pallas kernels, first(): pl.pallas_call(functools.partial(first_kernel, cap, slots), out_shape=(sh...  27.1 us
    pallas_call x1, Pallas kernels, second(): pl.pallas_call(functools.partial(second_kernel, cap, slots), out_shape=ja...  21.3 us

profile of v3, /device:TPU:2, one launch (start us, length us, event | category | flops | bytes accessed | tf_op | source)
XLA Modules:
  0.0 50.2 jit_solution(1863844205635068950)
XLA Ops:
  0.0 27.1 %gather_448.1 = (bf16[448,2048]{1,0:T(8,128)(2,1)S(1)}, f32[448,1]{1,0:T(8,128)S(1)}, bf16[2048,1280]{1,0:T(8,128)(2,1)S(1)}, bf16[2,8,4,16,128]{4,3,2,1,0:T(8,1...) custom-call(s32[9]{0:T(128)} %start_ref.1, s32[384]{0:T(512)} %irr_ref.1, ...), custom_call_target="tpu_custom_call" | custom-call | tf_op jit(solution)/shard_map/gather_448/pallas_call | solution.py:421
  27.7 21.6 %conditional.1 = (bf16[384,1280]{1,0:T(8,128)(2,1)S(1)}) conditional(s32[]{:T(128)} %bitcast.1, (s32[9]{0:T(128)}, s32[384]{0:T(512)}, bf16[64,384]{1,0:T(8,128)(2,1)}, bf16[1024,1280]{1,0:T(8,128)(2,1)}) %tuple.32, (s32[9]{0:T(128)}, bf16[448,2048]{1,0:T(8,128)(2,1)S(1)}, f32[448,1]{1,0:T(8,128)S(1)}, ...), branch_computations={%region_0.0_spmd, %region_1.0_spmd, %region_2.0_spmd, %region_3.0_... | conditional | bytes 8 | solution.py:478
  28.0 21.3 %exchange_352.1 = bf16[384,1280]{1,0:T(8,128)(2,1)S(1)} custom-call(s32[9]{0:T(128)} %get-tuple-element.92.start_ref, bf16[448,2048]{1,0:T(8,128)(2,1)S(1)} %get-tuple-element.93.lhs, f32[448,1]{1,0:T(8,128)S(1)} %get-tuple-element.94.low, bf16[2048,1280]{1,0:T(8,128)(2,1)S(1)} %get-tuple-element.95.ints, ...), custom_call_target="tpu_custom_call" | custom-call | tf_op jit(solution)/shard_map/cond/branch_2_fun/exchange_352/pallas_call | solution.py:445
  49.3 0.9 %copy.16 = bf16[384,1280]{1,0:T(8,128)(2,1)} copy(bf16[384,1280]{1,0:T(8,128)(2,1)S(1)} %get-tuple-element.127) | data formatting | bytes 1966080

commit v4 on v3

--- a/solution.py
+++ b/solution.py
@@ -18,7 +18,7 @@
 
 
 PART = 16
-SIZES = (256, 304, 352, 448)
+SIZES = (256, 304, 352, 416, 448)
 CAP = 128
 
 
@@ -31,7 +31,7 @@
         self.group = (1 - self.h) * 2 + self.core
         self.partner = self.at(1 - self.h, self.core, self.yh, self.x, self.z)
         self.sibling = self.at(self.h, 1 - self.core, self.yh, self.x, self.z)
-        self.near = [self.along_z(d) for d in (1, -1, 2, -2)] + [self.along_x(d) for d in (1, -1)]
+        self.near = [self.along_x(d) for d in (1, -1)]
 
     def at(self, h, core, yh, x, z):
         return (h * 2 + core, (yh * NX + x) * NZ + z)
@@ -85,11 +85,9 @@
         dst[:, pl.ds(b * 128, 128)] = full.astype(jnp.bfloat16)
 
 
-Z_PLAN = (
-    (0, 2, None), (0, -2, None), (0, 1, None), (0, -1, None),
-    (-2, 1, None), (2, -1, None), (-2, 2, 0), (2, -2, 1),
-)
-X_PLAN = ((0, 1, None), (0, -1, None), (-1, 1, 0), (1, -1, 1))
+Z_PLAN = tuple((0, d, None) for d in (4, 3, -3, 2, -2, 1, -1))
+X_PLAN = ((0, 1, 0), (0, -1, 1), (0, 1, 1), (0, -1, 0), (-1, 1, 0), (1, -1, 1))
+X_NEAR = 4
 
 
 def hop(place, axis, i, src, dst, send, recv, arriving=False):
@@ -106,9 +104,9 @@
 
 def first_kernel(
     cap, slots,
-    start_ref, irr_ref, amp_ref, int_ref,
+    start_hbm, irr_hbm, amp_hbm, int_ref,
     lhs, low, ints, gat_a, gat_b, irr_all, size_ref,
-    comp,
+    comp, start_ref, irr_ref, amp_ref, load_sem,
     irr_send, irr_recv, a_send, a_recv, b_send, b_recv, z_send, z_recv, x_send, x_recv,
     int_send, int_recv, own_sem, ready,
 ):
@@ -120,6 +118,13 @@
     kind = (p.h == p.yh).astype(jnp.int32)
     selfish = p.h == p.yh
 
+    loads = [
+        pltpu.make_async_copy(src, dst, load_sem.at[i])
+        for i, (src, dst) in enumerate(((irr_hbm, irr_ref), (start_hbm, start_ref), (amp_hbm, amp_ref)))
+    ]
+    for load in loads:
+        load.start()
+
     barrier = pltpu.get_barrier_semaphore()
 
     def signal(dev, inc=1):
@@ -130,7 +135,7 @@
         signal(p.sibling)
 
     signal(p.partner)
-    for dev in p.near:
+    for dev in p.near + [p.along_z(d) for _, d, _ in Z_PLAN]:
         signal(dev)
     for u in range(2):
         for d in range(1, NX):
@@ -144,6 +149,8 @@
 
     own_copy = pltpu.make_async_copy(int_ref, ints.at[pl.ds(p.core * depth, depth)], own_sem)
     own_copy.start()
+    for load in loads:
+        load.wait()
 
     mine = irr_ref[...].reshape(1, pairs)
     irr_all[p.pair] = mine
@@ -162,7 +169,7 @@
         gat_a[1, p.z, p.x] = block[:PART]
         gat_b[1, p.x, p.z] = block[PART:]
 
-    pl.semaphore_wait(barrier, 1 + len(p.near) + 2 * (NX + NZ - kind) + p.core)
+    pl.semaphore_wait(barrier, 1 + len(p.near) + len(Z_PLAN) + 2 * (NX + NZ - kind) + p.core)
 
     comp_a, comp_b = comp.at[pl.ds(0, PART)], comp.at[pl.ds(PART, rows - PART)]
 
@@ -250,22 +257,18 @@
         for d in range(NZ):
             arrival = remote(comp_b, gat_b.at[t, p.x, p.zs(d)], b_send.at[0], b_recv.at[t, p.zs(d)], p.partner)
             unless_own(t, d, arrival.wait_recv)
-        for i in range(2):
+        for i in range(X_NEAR):
             x_hop(t, i).start()
         for d in range(NX):
             arrival = remote(comp_a, gat_a.at[t, p.z, p.xs(d)], a_send.at[0], a_recv.at[t, p.xs(d)], p.partner)
             unless_own(t, d, arrival.wait_recv)
-        for i in range(4):
+        for i in range(len(Z_PLAN)):
             z_hop(t, i).start()
 
     gather_start(0)
     for i in range(2):
         x_hop(0, i, True).wait_recv()
-        x_hop(0, 2 + i).start()
-    for i in range(2):
-        z_hop(0, i, True).wait_recv()
-        z_hop(0, 4 + i).start()
-        z_hop(0, 6 + i).start()
+        x_hop(0, X_NEAR + i).start()
     gather_start(1)
 
     irr_arrival(1).wait_recv()
@@ -284,17 +287,17 @@
         choice = choice + jnp.where(most <= float(size), 1.0, 0.0)
     size_ref[0] = jnp.sum(choice).astype(jnp.int32)
 
-    for i in range(2, 4):
+    for i in range(2, len(X_PLAN)):
         x_hop(0, i, True).wait_recv()
-    for i in range(2, 8):
+    for i in range(len(Z_PLAN)):
         z_hop(0, i, True).wait_recv()
     expand(
         start_ref, p.h * half, half, pick,
         lambda zz, xx: gat_a[0, zz, xx], lambda xx, zz: gat_b[0, xx, zz], lhs,
     )
-    for i in range(2):
+    for i in range(X_NEAR):
         x_hop(1, i, True).wait_recv()
-    for i in range(4):
+    for i in range(len(Z_PLAN)):
         z_hop(1, i, True).wait_recv()
     own_copy.wait()
     int_arrival.wait_recv()
@@ -304,18 +307,18 @@
         irr_copy(k).wait_send()
     int_copy.wait_send()
     for t in range(2):
-        for i in range(4 if t else 8):
+        for i in range(len(Z_PLAN)):
             z_hop(t, i).wait_send()
-        for i in range(2 if t else 4):
+        for i in range(X_NEAR if t else len(X_PLAN)):
             x_hop(t, i).wait_send()
 
 
 def second_kernel(
     cap, slots,
-    start_ref, lhs, low, ints, gat_a, gat_b, irr_all,
+    start_hbm, lhs, low, ints, gat_a, gat_b, irr_all,
     out_ref,
-    slabs, columns, own, mix, acc, sendb, recvb,
-    z_send, z_recv, x_send, x_recv, ex_send, ex_recv,
+    start_ref, load_sem, columns, own, mix, acc, sendb, recvb,
+    x_send, x_recv, ex_send, ex_recv,
 ):
     p = Place()
     pairs = irr_all.shape[2]
@@ -325,6 +328,8 @@
     barrier = pltpu.get_barrier_semaphore()
     for dev in p.near + [p.partner]:
         pl.semaphore_signal(barrier, inc=1, device_id=dev, device_id_type=MESH)
+    load = pltpu.make_async_copy(start_hbm, start_ref, load_sem)
+    load.start()
 
     def span(j):
         return pl.ds(pl.multiple_of(j * TILE, TILE), TILE)
@@ -340,18 +345,17 @@
     product(0)
     pl.semaphore_wait(barrier, len(p.near) + 1)
 
-    def z_hop(i, arriving=False):
-        return hop(p, "z", i, gat_a.at[1], slabs, z_send.at[i - 4], z_recv.at[i - 4], arriving)
-
     def x_hop(i, arriving=False):
-        return hop(p, "x", i, gat_b.at[1], columns, x_send.at[i - 2], x_recv.at[i - 2], arriving)
-
-    for i in range(2, 4):
+        return hop(p, "x", i, gat_b.at[1], columns, x_send.at[i - X_NEAR], x_recv.at[i - X_NEAR], arriving)
+
+    for i in range(X_NEAR, len(X_PLAN)):
         x_hop(i).start()
-    for i in range(4, 8):
-        z_hop(i).start()
-
-    @pl.loop(1, tiles)
+
+    load.wait()
+    ex_copy(0).start()
+    product(1)
+
+    @pl.loop(2, tiles)
     def _(j):
         product(j)
         ex_copy(j - 1).start()
@@ -372,15 +376,11 @@
     mix[...] = jnp.where(jnp.logical_or(pos1 == slot, pos2 == slot), 1.0, 0.0).astype(jnp.bfloat16)
     pick = (mine_s * 512.0 + rank_s).astype(jnp.int32) - iota((pairs, cap), 1)
 
-    for d in range(-2, 3):
-        slabs[p.zs(d)] = gat_a[1, p.zs(d)]
     for d in range(-1, 2):
         columns[p.xs(d)] = gat_b[1, p.xs(d)]
-    for i in range(2, 4):
+    for i in range(X_NEAR, len(X_PLAN)):
         x_hop(i, True).wait_recv()
-    for i in range(4, 8):
-        z_hop(i, True).wait_recv()
-    expand(start_ref, p.h * half, half, pick, lambda zz, xx: slabs[zz, xx], lambda xx, zz: columns[xx, zz], own)
+    expand(start_ref, p.h * half, half, pick, lambda zz, xx: gat_a[1, zz, xx], lambda xx, zz: columns[xx, zz], own)
 
     @pl.loop(0, tiles)
     def _(j):
@@ -392,10 +392,8 @@
         total = acc[j] + jnp.dot(mix[...], recvb[j], preferred_element_type=F32)
         out_ref[:, span(j)] = total.astype(jnp.bfloat16)
 
-    for i in range(2, 4):
+    for i in range(X_NEAR, len(X_PLAN)):
         x_hop(i).wait_send()
-    for i in range(4, 8):
-        z_hop(i).wait_send()
 
     @pl.loop(0, tiles)
     def _(j):
@@ -404,6 +402,7 @@
 
 DMA = pltpu.SemaphoreType.DMA
 VMEM_SPEC = pl.BlockSpec(memory_space=pltpu.VMEM)
+ANY_SPEC = pl.BlockSpec(memory_space=pl.ANY)
 SMEM_SPEC = pl.BlockSpec(memory_space=pltpu.SMEM)
 
 
@@ -425,12 +424,13 @@
             shape((2, NZ, NX, PART, cap), bf16), shape((2, NX, NZ, rows - PART, cap), bf16),
             shape((4, 1, pairs), jnp.int32), shape((1,), jnp.int32),
         ),
-        in_specs=[SMEM_SPEC, VMEM_SPEC, VMEM_SPEC, pl.BlockSpec(memory_space=pl.ANY)],
+        in_specs=[ANY_SPEC] * 4,
         out_specs=(VMEM_SPEC,) * 6 + (SMEM_SPEC,),
         scratch_shapes=[
             pltpu.VMEM((rows, cap), bf16),
+            pltpu.SMEM(starts.shape, jnp.int32), pltpu.VMEM(irreps.shape, jnp.int32), pltpu.VMEM(amp.shape, bf16), DMA((3,)),
             DMA((3,)), DMA((3,)), DMA((2 * NX,)), DMA((2, NX)), DMA((2 * NZ,)), DMA((2, NZ)),
-            DMA((2, 8)), DMA((2, 8)), DMA((2, 4)), DMA((2, 4)),
+            DMA((2, len(Z_PLAN))), DMA((2, len(Z_PLAN))), DMA((2, len(X_PLAN))), DMA((2, len(X_PLAN))),
             DMA, DMA, DMA, pltpu.SemaphoreType.REGULAR,
         ],
         compiler_params=params(collective_id),
@@ -441,21 +441,22 @@
 def second(cap, slots, collective_id, starts, lhs, low, ints, gat_a, gat_b, irr_all):
     pairs, cols, half = irr_all.shape[2], ints.shape[1], ints.shape[0]
     tiles = cols // TILE
+    x_far = len(X_PLAN) - X_NEAR
     bf16 = jnp.bfloat16
     return pl.pallas_call(
         functools.partial(second_kernel, cap, slots),
         out_shape=jax.ShapeDtypeStruct((pairs, cols), bf16),
-        in_specs=[SMEM_SPEC] + [VMEM_SPEC] * 6,
+        in_specs=[ANY_SPEC] + [VMEM_SPEC] * 6,
         out_specs=VMEM_SPEC,
         scratch_shapes=[
-            pltpu.VMEM(gat_a.shape[1:], bf16),
+            pltpu.SMEM(starts.shape, jnp.int32), DMA,
             pltpu.VMEM(gat_b.shape[1:], bf16),
             pltpu.VMEM((pairs, half), bf16),
             pltpu.VMEM((pairs, slots), bf16),
             pltpu.VMEM((tiles, pairs, TILE), F32),
             pltpu.VMEM((tiles, slots, TILE), bf16),
             pltpu.VMEM((tiles, slots, TILE), bf16),
-            DMA((4,)), DMA((4,)), DMA((2,)), DMA((2,)), DMA((tiles,)), DMA((tiles,)),
+            DMA((x_far,)), DMA((x_far,)), DMA((tiles,)), DMA((tiles,)),
         ],
         compiler_params=params(collective_id),
         name="exchange_" + str(slots),

time: 50.9 us -> 43.1 us (0.85)
  Pallas kernels: 48.4 us -> 40.9 us
    pallas_call x1, Pallas kernels: 21.3 us -> 14.7 us  [second(): pl.pallas_call(functools.partial(second_kernel, cap, slots), out_shape=ja...]
    pallas_call x1, Pallas kernels: 27.1 us -> 26.2 us  [first(): pl.pallas_call(functools.partial(first_kernel, cap, slots), out_shape=(sh...]
where the time goes in v4:
time: 43.1 us; the launch traced here: 42.7 us
  Pallas kernels  40.9 us (95%)
  local copies, waits for them, and re-layouts  0.95 us (2%)
  between operations  0.64 us (1%)
    pallas_call x1, Pallas kernels, first(): pl.pallas_call(functools.partial(first_kernel, cap, slots), out_shape=(sh...  26.2 us
    pallas_call x1, Pallas kernels, second(): pl.pallas_call(functools.partial(second_kernel, cap, slots), out_shape=ja...  14.7 us
    unnamed x1, local copies, waits for them, and re-layouts  0.95 us

profile of v4, /device:TPU:2, one launch (start us, length us, event | category | flops | bytes accessed | tf_op | source)
XLA Modules:
  0.0 42.7 jit_solution(13826264302200503354)
XLA Ops:
  0.0 26.2 %gather_448.1 = (bf16[448,2048]{1,0:T(8,128)(2,1)S(1)}, f32[448,1]{1,0:T(8,128)S(1)}, bf16[2048,1280]{1,0:T(8,128)(2,1)S(1)}, bf16[2,8,4,16,128]{4,3,2,1,0:T(8,1...) custom-call(s32[9]{0:T(128)} %start_hbm.1, s32[384]{0:T(512)} %irr_hbm.1, ...), custom_call_target="tpu_custom_call" | custom-call | tf_op jit(solution)/shard_map/gather_448/pallas_call | solution.py:420
  26.8 15.0 %conditional.1 = (bf16[384,1280]{1,0:T(8,128)(2,1)S(1)}) conditional(s32[]{:T(128)} %bitcast.1, (s32[9]{0:T(128)}, s32[384]{0:T(512)}, bf16[64,384]{1,0:T(8,128)(2,1)}, bf16[1024,1280]{1,0:T(8,128)(2,1)}) %tuple.37, (s32[9]{0:T(128)}, bf16[448,2048]{1,0:T(8,128)(2,1)S(1)}, f32[448,1]{1,0:T(8,128)S(1)}, ...), branch_computations={%region_0.0_spmd, %region_1.0_spmd, %region_2.0_spmd, %region_3.0_... | conditional | bytes 8 | solution.py:479
  27.1 14.7 %exchange_256.1 = bf16[384,1280]{1,0:T(8,128)(2,1)S(1)} custom-call(s32[9]{0:T(128)} %get-tuple-element.128.start_hbm, bf16[448,2048]{1,0:T(8,128)(2,1)S(1)} %get-tuple-element.129.lhs, f32[448,1]{1,0:T(8,128)S(1)} %get-tuple-element.130.low, bf16[2048,1280]{1,0:T(8,128)(2,1)S(1)} %get-tuple-element.131.ints, ...), custom_call_target="tpu_custom_call" | custom-call | tf_op jit(solution)/shard_map/cond/branch_5_fun/exchange_256/pallas_call | solution.py:446
  41.8 0.9 %copy.18 = bf16[384,1280]{1,0:T(8,128)(2,1)} copy(bf16[384,1280]{1,0:T(8,128)(2,1)S(1)} %get-tuple-element.149) | data formatting | bytes 1966080
